TPU v7x, 128 devices: a whole 4x4x4 slice. The times are simulated.
128 devices in a mesh: bond: 8 (over x, core), op: 16 (over y, z).
Axes of the slice: x: 4, y: 4, z: 4, core: 2. Of those that a mesh axis runs over, the one named last changes fastest.
Arguments:
- wave_slab: bfloat16 [8192, 8192], P('op', 'bond'), may hold values from -6 to 6
- left_blocks: bfloat16 [32, 16, 2, 128, 128], P('op'), may hold values from -0.375 to 0.375
- right_blocks: bfloat16 [32, 64, 2, 128, 128], P('op'), may hold values from -0.0625 to 0.0625
- sector_size: int32 [64], replicated, may hold values from 1 to 128
- left_pairs: int32 [32, 16, 2], P('op'), may hold values from 0 to 63
- right_pairs: int32 [32, 64, 2], P('op'), may hold values from 0 to 63
Outputs:
- applied: float32 [2048, 8192], P('bond', 'op')
All inputs are finite; a program needn't handle non-finite values.
Results may differ from a plain program's by a relative error of at most 0.0029.
Values may be sent and summed in bfloat16 or wider, within the bound.
No kernel may reach another device: no remote copies, remote signals or barrier semaphores. Data moves between devices by JAX's collectives and lax.ppermute only.
A program may use at most 128 MiB of HBM per device.

v0:
```python
import jax
import jax.numpy as jnp
from jax import lax
from jax.sharding import PartitionSpec as P

TILE = 128


def live_mask(sector_size):
    states = jnp.arange(TILE, dtype=jnp.int32)
    return (states[None, :] < sector_size[:, None]).astype(jnp.float32).reshape(-1)


def on_device(wave_slab, left_blocks, right_blocks, sector_size, left_pairs, right_pairs):
    live = live_mask(sector_size)
    local_rows = wave_slab.shape[0]
    strip = wave_slab.shape[1]
    row_live = lax.dynamic_slice_in_dim(live, lax.axis_index("op") * local_rows, local_rows)
    col_live = lax.dynamic_slice_in_dim(live, lax.axis_index("bond") * strip, strip)
    masked = (wave_slab.astype(jnp.float32) * row_live[:, None] * col_live[None, :]).astype(
        jnp.bfloat16
    )
    whole = lax.all_gather(masked, "op", axis=0, tiled=True)
    full_width = whole.shape[0]
    sector_count = full_width // TILE
    sectors = whole.reshape(sector_count, TILE, strip)
    term_count = left_blocks.shape[0]
    middles = []
    for term_idx in range(term_count):
        picked = sectors[left_pairs[term_idx]]
        middle = jnp.einsum(
            "ipxy,ipys->ixs", left_blocks[term_idx], picked, preferred_element_type=jnp.float32
        )
        middles.append(middle.astype(jnp.bfloat16).reshape(-1, strip))
    stacked = jnp.stack(middles, 0)
    bond_count = lax.axis_size("bond")
    slab_rows = stacked.shape[1]
    share_rows = slab_rows // bond_count
    blocked = stacked.reshape(term_count, bond_count, share_rows, strip)
    arrived = lax.all_to_all(blocked, "bond", split_axis=1, concat_axis=3, tiled=True)
    row_count = arrived.shape[2]
    total = jnp.zeros((row_count, sector_count, TILE), jnp.float32)
    for term_idx in range(term_count):
        split_cols = arrived[term_idx, 0].reshape(row_count, sector_count, TILE)
        chosen = split_cols[:, right_pairs[term_idx]]
        total = total + jnp.einsum(
            "rjpy,jpyz->rjz", chosen, right_blocks[term_idx], preferred_element_type=jnp.float32
        )
    partial_value = total.reshape(row_count, full_width)
    summed = lax.psum_scatter(partial_value, "op", scatter_dimension=1, tiled=True)
    out_cols = summed.shape[1]
    out_row_live = lax.dynamic_slice_in_dim(live, lax.axis_index("bond") * share_rows, share_rows)
    out_col_live = lax.dynamic_slice_in_dim(live, lax.axis_index("op") * out_cols, out_cols)
    return summed * out_row_live[:, None] * out_col_live[None, :]


def solution(mesh):
    placed = (
        P("op", "bond"),
        P("op", None, None, None, None),
        P("op", None, None, None, None),
        P(),
        P("op", None, None),
        P("op", None, None),
    )
    return jax.shard_map(
        on_device, mesh=mesh, in_specs=placed, out_specs=P("bond", "op"), check_vma=False
    )
```

profile of v0, /device:TPU:0, one launch (start us, length us, event | category | flops | bytes accessed | tf_op | source)
XLA Modules:
  0.0 447.6 jit_solution(14537597451842649991)
XLA Ops:
  6.5 0.7 convert_bitcast_fusion
  7.4 2.5 multiply_convert_fusion
  9.9 0.7 compare_select_fusion.3
  11.0 112.9 %all-gather.2.cloned.1.call-done = bf16[8192,1024]{1,0:T(8,128)(2,1)} async-done(((bf16[512,1024]{1,0:T(8,128)(2,1)}), bf16[8192,1024]{1,0:T(8,128)(2,1)}) %all-gather.2.cloned.1.call-update) | async-done | bytes 16777232 | tf_op jit(solution)/shard_map/all_gather | solution.py:23
  123.9 10.9 %gather_fusion = bf16[32,128,1024]{2,1,0:T(8,128)(2,1)} fusion(bf16[64,128,1024]{2,1,0:T(8,128)(2,1)} %bitcast.83, s32[1024]{0:T(1024)S(1)} %pad_clamp_fusion.3), kind=kCustom, calls=%fused_computation | custom fusion | bytes 16777344 | tf_op jit(solution)/shard_map/gather | solution.py:30
  134.8 6.6 %bitcast_convert_fusion.1 = bf16[16,1024,128]{1,2,0:T(8,128)(2,1)} fusion(bf16[16,2,128,1024]{3,2,1,0:T(8,128)(2,1)} %bitcast.76, bf16[2,16,2,128,128]{4,3,2,1,0:T(8,128)(2,1)S(1)} %copy-done), kind=kOutput, calls=%fused_computation.7 | convolution fusion | flops 1075838976 | bytes 13631488 | tf_op jit(solution)/shard_map/ipxy,ipys->ixs/dot_general | solution.py:31
  141.4 6.4 %copy.27 = bf16[1,8,256,1024]{2,3,0,1:T(8,128)(2,1)} copy(bf16[1,8,256,1024]{3,2,1,0:T(8,128)(2,1)} %bitcast.81) | data formatting | bytes 8388608 | tf_op jit(solution)/shard_map/stack | solution.py:35
  147.8 10.8 %gather_fusion.1 = bf16[32,128,1024]{2,1,0:T(8,128)(2,1)} fusion(bf16[64,128,1024]{2,1,0:T(8,128)(2,1)} %bitcast.84, s32[1024]{0:T(1024)S(1)} %pad_clamp_fusion.2), kind=kCustom, calls=%fused_computation.1 | custom fusion | bytes 16777344 | tf_op jit(solution)/shard_map/gather | solution.py:30
  158.6 6.6 %bitcast_convert_fusion = bf16[16,1024,128]{1,2,0:T(8,128)(2,1)} fusion(bf16[16,2,128,1024]{3,2,1,0:T(8,128)(2,1)} %bitcast.75, bf16[2,16,2,128,128]{4,3,2,1,0:T(8,128)(2,1)S(1)} %copy-done), kind=kOutput, calls=%fused_computation.6 | convolution fusion | flops 1075838976 | bytes 13631488 | tf_op jit(solution)/shard_map/ipxy,ipys->ixs/dot_general | solution.py:31
  165.2 6.5 %copy.28 = bf16[1,8,256,1024]{2,3,0,1:T(8,128)(2,1)} copy(bf16[1,8,256,1024]{3,2,1,0:T(8,128)(2,1)} %bitcast.82) | data formatting | bytes 8388608 | tf_op jit(solution)/shard_map/stack | solution.py:35
  171.7 7.5 %pad_maximum_fusion = bf16[2,8,256,1024]{2,3,0,1:T(8,128)(2,1)} fusion(bf16[1,8,256,1024]{2,3,0,1:T(8,128)(2,1)} %copy.28, bf16[1,8,256,1024]{2,3,0,1:T(8,128)(2,1)} %copy.27), kind=kLoop, calls=%fused_computation.4 | loop fusion | flops 4194304 | bytes 16777216 | tf_op jit(solution)/shard_map/stack | solution.py:35
  179.1 5.2 %all-to-all-start = ((bf16[2,8,256,1024]{2,3,0,1:T(8,128)(2,1)}), bf16[2,8,256,1024]{2,3,0,1:T(8,128)(2,1)}, u32[]{:S(2)}, u32[]{:S(2)}) async-start(bf16[2,8,256,1024]{2,3,0,1:T(8,128)(2,1)} %pad_maximum_fusion), calls=%async_computation | async-start | bytes 16777216 | tf_op jit(solution)/shard_map/all_to_all | solution.py:40
  185.0 93.8 %all-to-all-done = bf16[2,8,256,1024]{2,3,0,1:T(8,128)(2,1)} async-done(((bf16[2,8,256,1024]{2,3,0,1:T(8,128)(2,1)}), bf16[2,8,256,1024]{2,3,0,1:T(8,128)(2,1)}, u32[]{:S(2)}, u32[]{:S(2)}) %all-to-all-start) | async-done | bytes 8388640 | tf_op jit(solution)/shard_map/all_to_all | solution.py:40
  278.9 7.3 %copy.44 = bf16[2,8,256,1024]{2,3,1,0:T(8,128)(2,1)} copy(bf16[2,8,256,1024]{2,3,0,1:T(8,128)(2,1)} %all-to-all-done) | data formatting | bytes 16777216 | tf_op jit(solution)/shard_map/all_to_all | solution.py:40
  286.2 5.7 %fusion.12 = (bf16[1,1,256,8,1024]{2,4,3,1,0:T(8,128)(2,1)}, bf16[1,1,256,8,1024]{2,4,3,1,0:T(8,128)(2,1)}) fusion(bf16[2,1,256,8,1024]{2,4,3,1,0:T(8,128)(2,1)} %bitcast.79), kind=kLoop, calls=%fused_computation.31 | loop fusion | bytes 16777216 | tf_op jit(solution)/shard_map/slice | solution.py:44
  291.9 6.4 %copy.34 = bf16[256,64,128]{2,0,1:T(8,128)(2,1)} copy(bf16[256,64,128]{0,2,1:T(8,128)(2,1)} %bitcast.86) | data formatting | bytes 8388608 | tf_op jit(solution)/shard_map/reshape;squeeze | solution.py:44
  298.3 6.3 %copy.31 = bf16[256,64,128]{2,0,1:T(8,128)(2,1)} copy(bf16[256,64,128]{0,2,1:T(8,128)(2,1)} %bitcast.85) | data formatting | bytes 8388608 | tf_op jit(solution)/shard_map/reshape;squeeze | solution.py:44
  304.6 8.8 %gather_fusion.3 = bf16[128,256,128]{2,1,0:T(8,128)(2,1)} fusion(bf16[256,64,128]{2,0,1:T(8,128)(2,1)} %copy.34, s32[1024]{0:T(1024)S(1)} %pad_clamp_fusion), kind=kCustom, calls=%fused_computation.3 | custom fusion | bytes 16777728 | tf_op jit(solution)/shard_map/gather | solution.py:45
  313.4 10.7 %fusion = f32[64,256,128,1]{1,2,3,0:T(8,128)} fusion(bf16[256,64,2,128]{3,0,2,1:T(8,128)(2,1)} %bitcast.80, bf16[2,64,2,128,128]{4,3,2,1,0:T(8,128)(2,1)} %param.8), kind=kOutput, calls=%fused_computation.9 | convolution fusion | flops 1073741824 | bytes 20971520 | tf_op jit(solution)/shard_map/rjpy,jpyz->rjz/dot_general | solution.py:46
  324.1 8.8 %gather_fusion.2 = bf16[128,256,128]{2,1,0:T(8,128)(2,1)} fusion(bf16[256,64,128]{2,0,1:T(8,128)(2,1)} %copy.31, s32[1024]{0:T(1024)S(1)} %pad_clamp_fusion.1), kind=kCustom, calls=%fused_computation.2 | custom fusion | bytes 16777728 | tf_op jit(solution)/shard_map/gather | solution.py:45
  332.8 13.2 %bitcast_add_fusion = f32[64,256,128]{1,2,0:T(8,128)} fusion(f32[64,256,128,1]{1,2,3,0:T(8,128)} %fusion, bf16[256,64,2,128]{3,0,2,1:T(8,128)(2,1)} %bitcast.77, bf16[2,64,2,128,128]{4,3,2,1,0:T(8,128)(2,1)} %param.8), kind=kOutput, calls=%fused_computation.5 | convolution fusion | flops 1075838976 | bytes 29360128 | tf_op jit(solution)/shard_map/rjpy,jpyz->rjz/dot_general | solution.py:46
  346.0 8.9 %copy.36 = f32[256,8192]{1,0:T(8,128)} copy(f32[256,8192]{0,1:T(8,128)} %bitcast.78) | data formatting | bytes 16777216 | tf_op jit(solution)/shard_map/reshape | solution.py:49
  355.0 83.9 %reduce-scatter.2.cloned.1.call-done = f32[256,512]{1,0:T(8,128)} async-done(((f32[256,8192]{1,0:T(8,128)}), f32[256,512]{1,0:T(8,128)}) %reduce-scatter.2.cloned.1.call-update) | async-done | bytes 524304 | tf_op jit(solution)/shard_map/reduce_scatter | solution.py:50
  438.9 1.9 multiply_multiply_fusion
  (24 shorter events, 1.3 us)
Async XLA Ops:
  6.5 117.3 %all-gather.2.cloned.1.call-start = ((), (), s32[]{:S(2)}) async-start(), calls=%async_computation.2 | async-start | bytes 17825792 | tf_op jit(solution)/shard_map/all_gather | solution.py:23
  123.9 10.9 %copy-start = (bf16[2,16,2,128,128]{4,3,2,1,0:T(8,128)(2,1)S(1)}, bf16[2,16,2,128,128]{4,3,2,1,0:T(8,128)(2,1)}, u32[]{:S(2)}) copy-start(bf16[2,16,2,128,128]{4,3,2,1,0:T(8,128)(2,1)} %param.7) | copy-start | bytes 6291460
  179.1 5.4 %copy-start.1 = (s32[2,64,2]{1,2,0:T(2,128)S(1)}, s32[2,64,2]{1,2,0:T(2,128)}, u32[]{:S(2)}) copy-start(s32[2,64,2]{1,2,0:T(2,128)} %param.11) | copy-start | bytes 3076
  179.1 99.8 %all-to-all-start = ((bf16[2,8,256,1024]{2,3,0,1:T(8,128)(2,1)}), bf16[2,8,256,1024]{2,3,0,1:T(8,128)(2,1)}, u32[]{:S(2)}, u32[]{:S(2)}) async-start(bf16[2,8,256,1024]{2,3,0,1:T(8,128)(2,1)} %pad_maximum_fusion), calls=%async_computation | async-start | bytes 16777216 | tf_op jit(solution)/shard_map/all_to_all | solution.py:40
  184.3 254.6 %reduce-scatter.2.cloned.1.call-start = ((), (), s32[]{:S(2)}) async-start(), calls=%async_computation.3 | async-start | bytes 8912896 | tf_op jit(solution)/shard_map/reduce_scatter | solution.py:50
Sparse Core Ops, SparseCore 0:
  10.0 113.8 all-gather.1
  355.0 83.7 reduce-scatter.1
where the time goes:
time: 449 us; the launch traced here: 448 us
  waiting for transfers between devices  291 us (65%)
  local copies, waits for them, and re-layouts  87.8 us (20%)
  matrix products  37 us (8%)
  between operations  13.5 us (3%)
  other arithmetic  13.4 us (3%)
  starting transfers between devices  5.4 us (1%)
    all_gather x1, waiting for transfers between devices, on_device(): whole = lax.all_gather(masked, 'op', axis=0, tiled=True)  113 us
    all_to_all x1, waiting for transfers between devices, on_device(): lax.all_to_all(blocked, 'bond', split_axis=1, concat_axis=3, tiled=True)  93.8 us
    reduce_scatter x1, waiting for transfers between devices, on_device(): lax.psum_scatter(partial_value, 'op', scatter_dimension=1, tiled=True)  83.9 us
    dot_general x2, matrix products, on_device(): jnp.einsum('rjpy,jpyz->rjz', chosen, right_blocks[term_idx], preferred_el...  23.8 us
    gather x2, local copies, waits for them, and re-layouts, on_device(): picked = sectors[left_pairs[term_idx]]  21.7 us
    gather x2, local copies, waits for them, and re-layouts, on_device(): chosen = split_cols[:, right_pairs[term_idx]]  17.6 us
    dot_general x2, matrix products, on_device(): jnp.einsum('ipxy,ipys->ixs', left_blocks[term_idx], picked, preferred_ele...  13.2 us
    another operation x2, local copies, waits for them, and re-layouts, on_device(): stacked = jnp.stack(middles, 0)  12.9 us
  transfers between devices with their start and end apart: 3, of which 3 were waited for; matrix products, arithmetic and copies ran while one was open for 0% of the time, Pallas kernels for 0%

commit v1 on v0

--- a/solution.py
+++ b/solution.py
@@ -2,8 +2,15 @@
 import jax.numpy as jnp
 from jax import lax
 from jax.sharding import PartitionSpec as P
+from jax.lax import all_to_all, axis_size
 
 TILE = 128
+
+
+def read_edge(local_values):
+    return jnp.concatenate(
+        all_to_all(jnp.stack([local_values] * axis_size("op"), axis=0), "op", 0, 0), axis=0
+    )
 
 
 def live_mask(sector_size):
@@ -20,7 +27,7 @@
     masked = (wave_slab.astype(jnp.float32) * row_live[:, None] * col_live[None, :]).astype(
         jnp.bfloat16
     )
-    whole = lax.all_gather(masked, "op", axis=0, tiled=True)
+    whole = read_edge(masked)
     full_width = whole.shape[0]
     sector_count = full_width // TILE
     sectors = whole.reshape(sector_count, TILE, strip)

time: 449 us -> 648 us (1.44)
  waiting for transfers between devices: 291 us -> 477 us
  starting transfers between devices: 5.4 us -> 13.7 us
    all_to_all x0 -> x1, waiting for transfers between devices: none -> 293 us  [read_edge(): all_to_all(jnp.stack([local_values] * axis_size('op'), axis=0), 'op', 0, 0)]
    all_gather x1 -> x0, waiting for transfers between devices: 113 us -> none  [on_device(): whole = lax.all_gather(masked, 'op', axis=0, tiled=True)]
    all_to_all x0 -> x1, starting transfers between devices: none -> 8.34 us  [read_edge(): all_to_all(jnp.stack([local_values] * axis_size('op'), axis=0), 'op', 0, 0)]
where the time goes in v1:
time: 648 us; the launch traced here: 646 us
  waiting for transfers between devices  477 us (74%)
  local copies, waits for them, and re-layouts  93.8 us (14%)
  matrix products  37 us (6%)
  starting transfers between devices  13.7 us (2%)
  between operations  13.5 us (2%)
  other arithmetic  11.7 us (2%)
    all_to_all x1, waiting for transfers between devices, read_edge(): all_to_all(jnp.stack([local_values] * axis_size('op'), axis=0), 'op', 0, 0)  293 us
    all_to_all x1, waiting for transfers between devices, on_device(): lax.all_to_all(blocked, 'bond', split_axis=1, concat_axis=3, tiled=True)  93.8 us
    reduce_scatter x1, waiting for transfers between devices, on_device(): lax.psum_scatter(partial_value, 'op', scatter_dimension=1, tiled=True)  89.2 us
    dot_general x2, matrix products, on_device(): jnp.einsum('rjpy,jpyz->rjz', chosen, right_blocks[term_idx], preferred_el...  23.8 us
    gather x2, local copies, waits for them, and re-layouts, on_device(): picked = sectors[left_pairs[term_idx]]  21.7 us
    gather x2, local copies, waits for them, and re-layouts, on_device(): chosen = split_cols[:, right_pairs[term_idx]]  17.6 us
    dot_general x2, matrix products, on_device(): jnp.einsum('ipxy,ipys->ixs', left_blocks[term_idx], picked, preferred_ele...  13.2 us
  transfers between devices with their start and end apart: 3, of which 3 were waited for; matrix products, arithmetic and copies ran while one was open for 0% of the time, Pallas kernels for 0%

profile of v1, /device:TPU:0, one launch (start us, length us, event | category | flops | bytes accessed | tf_op | source)
XLA Modules:
  0.0 646.4 jit_solution(1902881723506891156)
XLA Ops:
  7.3 1.5 multiply_convert_fusion
  8.9 6.0 stack.8
  14.9 8.3 %all-to-all-start = ((bf16[16,512,1024]{2,1,0:T(8,128)(2,1)}), bf16[16,512,1024]{2,1,0:T(8,128)(2,1)}, u32[]{:S(2)}, u32[]{:S(2)}) async-start(bf16[16,512,1024]{2,1,0:T(8,128)(2,1)} %stack.8), calls=%async_computation | async-start | bytes 33554432 | tf_op jit(solution)/shard_map/all_to_all | solution.py:12
  23.7 293.5 %all-to-all-done = bf16[16,512,1024]{2,1,0:T(8,128)(2,1)} async-done(((bf16[16,512,1024]{2,1,0:T(8,128)(2,1)}), bf16[16,512,1024]{2,1,0:T(8,128)(2,1)}, u32[]{:S(2)}, u32[]{:S(2)}) %all-to-all-start) | async-done | bytes 16777248 | tf_op jit(solution)/shard_map/all_to_all | solution.py:12
  317.2 10.8 %gather_fusion.1 = bf16[32,128,1024]{2,1,0:T(8,128)(2,1)} fusion(bf16[64,128,1024]{2,1,0:T(8,128)(2,1)} %bitcast.1, s32[1024]{0:T(1024)S(1)} %pad_clamp_fusion.2), kind=kCustom, calls=%fused_computation.1 | custom fusion | bytes 16777344 | tf_op jit(solution)/shard_map/gather | solution.py:37
  327.9 10.9 %gather_fusion = bf16[32,128,1024]{2,1,0:T(8,128)(2,1)} fusion(bf16[64,128,1024]{2,1,0:T(8,128)(2,1)} %bitcast.1, s32[1024]{0:T(1024)S(1)} %pad_clamp_fusion.3), kind=kCustom, calls=%fused_computation | custom fusion | bytes 16777344 | tf_op jit(solution)/shard_map/gather | solution.py:37
  338.9 6.6 %bitcast_convert_fusion.1 = bf16[16,1024,128]{1,2,0:T(8,128)(2,1)} fusion(bf16[16,2,128,1024]{3,2,1,0:T(8,128)(2,1)} %bitcast.76, bf16[2,16,2,128,128]{4,3,2,1,0:T(8,128)(2,1)S(1)} %copy-done), kind=kOutput, calls=%fused_computation.7 | convolution fusion | flops 1075838976 | bytes 13631488 | tf_op jit(solution)/shard_map/ipxy,ipys->ixs/dot_general | solution.py:38
  345.5 6.5 copy.27
  351.9 6.6 %bitcast_convert_fusion = bf16[16,1024,128]{1,2,0:T(8,128)(2,1)} fusion(bf16[16,2,128,1024]{3,2,1,0:T(8,128)(2,1)} %bitcast.75, bf16[2,16,2,128,128]{4,3,2,1,0:T(8,128)(2,1)S(1)} %copy-done), kind=kOutput, calls=%fused_computation.6 | convolution fusion | flops 1075838976 | bytes 13631488 | tf_op jit(solution)/shard_map/ipxy,ipys->ixs/dot_general | solution.py:38
  358.5 6.5 copy.28
  365.0 7.5 %pad_maximum_fusion = bf16[2,8,256,1024]{2,3,0,1:T(8,128)(2,1)} fusion(bf16[1,8,256,1024]{2,3,0,1:T(8,128)(2,1)} %copy.28, bf16[1,8,256,1024]{2,3,0,1:T(8,128)(2,1)} %copy.27), kind=kLoop, calls=%fused_computation.4 | loop fusion | flops 4194304 | bytes 16777216 | tf_op jit(solution)/shard_map/stack | solution.py:42
  372.4 5.2 all-to-all-start.1
  378.4 93.8 %all-to-all-done.1 = bf16[2,8,256,1024]{2,3,0,1:T(8,128)(2,1)} async-done(((bf16[2,8,256,1024]{2,3,0,1:T(8,128)(2,1)}), bf16[2,8,256,1024]{2,3,0,1:T(8,128)(2,1)}, u32[]{:S(2)}, u32[]{:S(2)}) %all-to-all-start.1) | async-done | bytes 8388640 | tf_op jit(solution)/shard_map/all_to_all | solution.py:47
  472.2 7.3 %copy.44 = bf16[2,8,256,1024]{2,3,1,0:T(8,128)(2,1)} copy(bf16[2,8,256,1024]{2,3,0,1:T(8,128)(2,1)} %all-to-all-done.1) | data formatting | bytes 16777216 | tf_op jit(solution)/shard_map/all_to_all | solution.py:47
  479.5 5.7 fusion.12
  485.2 6.3 copy.31
  491.6 6.4 copy.34
  497.9 8.8 %gather_fusion.3 = bf16[128,256,128]{2,1,0:T(8,128)(2,1)} fusion(bf16[256,64,128]{2,0,1:T(8,128)(2,1)} %copy.34, s32[1024]{0:T(1024)S(1)} %pad_clamp_fusion), kind=kCustom, calls=%fused_computation.3 | custom fusion | bytes 16777728 | tf_op jit(solution)/shard_map/gather | solution.py:52
  506.7 10.7 %fusion = f32[64,256,128,1]{1,2,3,0:T(8,128)} fusion(bf16[256,64,2,128]{3,0,2,1:T(8,128)(2,1)} %bitcast.80, bf16[2,64,2,128,128]{4,3,2,1,0:T(8,128)(2,1)} %param.8), kind=kOutput, calls=%fused_computation.9 | convolution fusion | flops 1073741824 | bytes 20971520 | tf_op jit(solution)/shard_map/rjpy,jpyz->rjz/dot_general | solution.py:53
  517.4 8.8 %gather_fusion.2 = bf16[128,256,128]{2,1,0:T(8,128)(2,1)} fusion(bf16[256,64,128]{2,0,1:T(8,128)(2,1)} %copy.31, s32[1024]{0:T(1024)S(1)} %pad_clamp_fusion.1), kind=kCustom, calls=%fused_computation.2 | custom fusion | bytes 16777728 | tf_op jit(solution)/shard_map/gather | solution.py:52
  526.2 13.2 %bitcast_add_fusion = f32[64,256,128]{1,2,0:T(8,128)} fusion(f32[64,256,128,1]{1,2,3,0:T(8,128)} %fusion, bf16[256,64,2,128]{3,0,2,1:T(8,128)(2,1)} %bitcast.77, bf16[2,64,2,128,128]{4,3,2,1,0:T(8,128)(2,1)} %param.8), kind=kOutput, calls=%fused_computation.5 | convolution fusion | flops 1075838976 | bytes 29360128 | tf_op jit(solution)/shard_map/rjpy,jpyz->rjz/dot_general | solution.py:53
  539.3 8.9 %copy.36 = f32[256,8192]{1,0:T(8,128)} copy(f32[256,8192]{0,1:T(8,128)} %bitcast.78) | data formatting | bytes 16777216 | tf_op jit(solution)/shard_map/reshape | solution.py:56
  548.3 89.2 %reduce-scatter.2.cloned.1.call-done = f32[256,512]{1,0:T(8,128)} async-done(((f32[256,8192]{1,0:T(8,128)}), f32[256,512]{1,0:T(8,128)}) %reduce-scatter.2.cloned.1.call-update) | async-done | bytes 524304 | tf_op jit(solution)/shard_map/reduce_scatter | solution.py:57
  637.6 1.9 multiply_multiply_fusion
  (26 shorter events, 2.0 us)
Async XLA Ops:
  14.9 8.4 %copy-start.1 = (s32[2,16,2]{1,2,0:T(2,128)S(1)}, s32[2,16,2]{1,2,0:T(2,128)}, u32[]{:S(2)}) copy-start(s32[2,16,2]{1,2,0:T(2,128)} %param.10) | copy-start | bytes 772
  14.9 302.2 %all-to-all-start = ((bf16[16,512,1024]{2,1,0:T(8,128)(2,1)}), bf16[16,512,1024]{2,1,0:T(8,128)(2,1)}, u32[]{:S(2)}, u32[]{:S(2)}) async-start(bf16[16,512,1024]{2,1,0:T(8,128)(2,1)} %stack.8), calls=%async_computation | async-start | bytes 33554432 | tf_op jit(solution)/shard_map/all_to_all | solution.py:12
  327.9 10.9 %copy-start = (bf16[2,16,2,128,128]{4,3,2,1,0:T(8,128)(2,1)S(1)}, bf16[2,16,2,128,128]{4,3,2,1,0:T(8,128)(2,1)}, u32[]{:S(2)}) copy-start(bf16[2,16,2,128,128]{4,3,2,1,0:T(8,128)(2,1)} %param.7) | copy-start | bytes 6291460
  372.4 5.4 copy-start.2
  372.4 99.8 %all-to-all-start.1 = ((bf16[2,8,256,1024]{2,3,0,1:T(8,128)(2,1)}), bf16[2,8,256,1024]{2,3,0,1:T(8,128)(2,1)}, u32[]{:S(2)}, u32[]{:S(2)}) async-start(bf16[2,8,256,1024]{2,3,0,1:T(8,128)(2,1)} %pad_maximum_fusion), calls=%async_computation.1 | async-start | bytes 16777216 | tf_op jit(solution)/shard_map/all_to_all | solution.py:47
  377.6 260.0 %reduce-scatter.2.cloned.1.call-start = ((), (), s32[]{:S(2)}) async-start(), calls=%async_computation.3 | async-start | bytes 8912896 | tf_op jit(solution)/shard_map/reduce_scatter | solution.py:57
Sparse Core Ops, SparseCore 0:
  548.4 89.1 reduce-scatter.1
